TPU v7x, 256 devices: a whole 4x4x8 slice. The times are simulated.
256 devices in a mesh: dp: 32 (over y, z_lo, core), cent: 8 (over x, z_hi).
Axes of the slice: x: 4, y: 4, z: 8 (z_hi: 2, z_lo: 4; z = z_hi * 4 + z_lo), core: 2. Of those that a mesh axis runs over, the one named last changes fastest.
Arguments:
- hidden: bfloat16 [5632, 11008], P('dp', 'cent'), may hold values from -6 to 6
- residual: bfloat16 [5632, 4096], P('dp', 'cent'), may hold values from -6 to 6
- down_weight: bfloat16 [11008, 4096], P('cent', 'dp'), may hold values from -0.0546875 to 0.0546875
- gain: float32 [4096], P('cent'), may hold values from 0.1 to 1.9
- proj_weight: bfloat16 [4096, 1024], P('cent'), may hold values from -0.09375 to 0.09375
- centroids: bfloat16 [131072, 1024], P(('dp', 'cent')), may hold values from -24 to 24
Outputs:
- weighted: float32 [131072, 1024], P(('dp', 'cent'))
- counts: float32 [131072], P(('dp', 'cent'))
All inputs are finite; a program needn't handle non-finite values.
Results may differ from a plain program's by a relative error of at most 0.011.
Values may be sent and summed in bfloat16 or wider, within the bound.
A program may use at most 128 MiB of HBM per device.

v0:
```python
import math
import jax
import jax.numpy as jnp
from jax import lax
from jax.sharding import PartitionSpec as P


def body(hidden, residual, down_weight, gain, proj_weight, centroids):
    partial_layer = jnp.dot(
        hidden,
        lax.all_gather(down_weight, "dp", axis=1, tiled=True),
        preferred_element_type=jnp.float32,
    )
    layer_out = lax.psum_scatter(partial_layer, "cent", scatter_dimension=1, tiled=True)
    normed = ((layer_out + residual.astype(jnp.float32)) * gain).astype(jnp.bfloat16)
    partial_embed = jnp.dot(normed, proj_weight, preferred_element_type=jnp.float32)
    embed_width = proj_weight.shape[1]
    embed_full = lax.psum(partial_embed, "cent")
    scaled = (
        embed_full * lax.rsqrt(jnp.mean(embed_full * embed_full, axis=1, keepdims=True) + 1e-06)
    ).astype(jnp.bfloat16)
    gathered = lax.all_gather(scaled, "dp", axis=0, tiled=True)
    inverse = 1.0 / (math.sqrt(embed_width) * 0.05)
    scores = (
        lax.dot_general(
            gathered, centroids, (((1,), (1,)), ((), ())), preferred_element_type=jnp.float32
        )
        * inverse
    )
    local_max = jnp.max(scores, axis=1)
    row_max = lax.pmax(local_max, ("dp", "cent"))
    row_total = lax.psum(jnp.sum(jnp.exp(scores - row_max[:, None]), axis=1), ("dp", "cent"))
    log_total = row_max + jnp.log(row_total)
    probability = jnp.exp(scores - log_total[:, None])
    scale_up = centroids.shape[0] * lax.axis_size("dp") * lax.axis_size("cent") / gathered.shape[0]
    counts = scale_up * jnp.sum(probability, axis=0)
    prob_low = probability.astype(jnp.bfloat16)
    weighted = scale_up * lax.dot_general(
        prob_low, gathered, (((0,), (0,)), ((), ())), preferred_element_type=jnp.float32
    )
    return (weighted, counts)


def solution(mesh):
    in_specs = (
        P("dp", "cent"),
        P("dp", "cent"),
        P("cent", "dp"),
        P("cent"),
        P("cent", None),
        P(("dp", "cent"), None),
    )
    out_specs = (P(("dp", "cent"), None), P(("dp", "cent")))
    return jax.shard_map(body, mesh=mesh, in_specs=in_specs, out_specs=out_specs, check_vma=False)
```

profile of v0, /device:TPU:1, one launch (start us, length us, event | category | flops | bytes accessed | tf_op | source)
XLA Modules:
  0.0 617.1 jit_solution(13492038344672853306)
XLA Ops:
  7.2 0.0 copy-start
  7.2 0.0 copy-start.1
  7.2 0.0 copy-start.3
  7.2 0.0 copy-start.2
  7.2 0.0 all-gather.3.cloned.1.call-start
  7.3 0.7 all-gather.3.cloned.1.call-update
  7.9 0.0 reduce-scatter.2.cloned.1.call-start
  8.0 105.2 %all-gather.3.cloned.1.call-done = bf16[1376,4096]{1,0:T(8,128)(2,1)} async-done(((bf16[1376,128]{1,0:T(8,128)(2,1)}), bf16[1376,4096]{1,0:T(8,128)(2,1)}) %all-gather.3.cloned.1.call-update) | async-done | bytes 11272208 | tf_op jit(solution)/shard_map/all_gather | solution.py:11
  113.2 8.5 %fusion.11 = f32[176,4096]{1,0:T(8,128)} fusion(bf16[176,1376]{1,0:T(8,128)(2,1)} %param.6, bf16[1376,4096]{1,0:T(8,128)(2,1)} %all-gather.3.cloned.1.call-done), kind=kOutput, calls=%fused_computation.17 | convolution fusion | flops 1983905792 | bytes 14640128 | tf_op jit(solution)/shard_map/dot_general | solution.py:9
  121.7 0.0 reduce-scatter.2.cloned.1.call-update
  121.7 0.0 all-reduce.2.cloned.1.call-start
  121.8 103.8 %reduce-scatter.2.cloned.1.call-done = f32[176,512]{1,0:T(8,128)} async-done(((f32[176,4096]{1,0:T(8,128)}), f32[176,512]{1,0:T(8,128)}) %reduce-scatter.2.cloned.1.call-update) | async-done | bytes 360464 | tf_op jit(solution)/shard_map/reduce_scatter | solution.py:14
  225.6 0.0 copy-done.1
  225.6 0.0 copy-done.3
  225.6 0.0 copy-done.2
  225.6 2.2 fusion.8
  227.8 0.0 all-reduce.2.cloned.1.call-update
  227.8 0.0 all-gather.5.cloned.1.call-start
  227.8 112.2 %all-reduce.2.cloned.1.call-done = f32[176,1024]{1,0:T(8,128)} async-done(((f32[176,1024]{1,0:T(8,128)}), f32[176,1024]{1,0:T(8,128)}) %all-reduce.2.cloned.1.call-update) | async-done | bytes 720912 | tf_op jit(solution)/shard_map/psum | solution.py:18
  340.1 1.2 multiply_reduce_fusion
  341.3 2.0 multiply_convert_fusion
  343.3 0.0 all-gather.5.cloned.1.call-update
  343.3 78.9 %all-gather.5.cloned.1.call-done = bf16[5632,1024]{1,0:T(8,128)(2,1)} async-done(((bf16[176,1024]{1,0:T(8,128)(2,1)}), bf16[5632,1024]{1,0:T(8,128)(2,1)}) %all-gather.5.cloned.1.call-update) | async-done | bytes 11534352 | tf_op jit(solution)/shard_map/all_gather | solution.py:22
  422.2 0.0 copy-done
  422.2 13.2 %fusion.10 = (f32[5632]{0:T(1024)S(1)}, f32[5632,512]{0,1:T(8,128)}) fusion(bf16[5632,1024]{1,0:T(8,128)(2,1)} %all-gather.5.cloned.1.call-done, bf16[512,1024]{1,0:T(8,128)(2,1)S(1)} %copy-done), kind=kOutput, calls=%fused_computation.16 | convolution fusion | flops 5911341568 | bytes 24139776 | tf_op jit(solution)/shard_map/dot_general | solution.py:25
  435.3 76.1 %pmax.7 = f32[5632]{0:T(1024)S(1)} all-reduce(f32[5632]{0:T(1024)S(1)} %get-tuple-element.2), channel_id=1, replica_groups=mesh['dp'=32,'cent'=8] {'dp','cent'}, use_global_device_ids=true, to_apply=%region_4.0 | all-reduce | flops 5632 | bytes 45056 | tf_op jit(solution)/shard_map/pmax | solution.py:31
  511.4 6.0 exponential_reduce_fusion
  517.4 73.3 %psum.15 = f32[5632]{0:T(1024)S(1)} all-reduce(f32[5632]{0:T(1024)S(1)} %exponential_reduce_fusion), channel_id=1, replica_groups=mesh['dp'=32,'cent'=8] {'dp','cent'}, use_global_device_ids=true, to_apply=%region_6.0 | all-reduce | flops 5632 | bytes 45056 | tf_op jit(solution)/shard_map/psum | solution.py:32
  590.7 6.0 fusion
  596.7 0.6 broadcast_multiply_fusion
  597.3 13.3 %fusion.5 = f32[512,1024]{1,0:T(8,128)} fusion(bf16[5632,1024]{1,0:T(8,128)(2,1)} %all-gather.5.cloned.1.call-done, f32[5632,512]{0,1:T(8,128)} %get-tuple-element.3, f32[5632]{0:T(1024)S(1)} %log_add_fusion), kind=kOutput, calls=%fused_computation.7 | convolution fusion | flops 5911871488 | bytes 25188352 | tf_op jit(solution)/shard_map/dot_general | solution.py:38
  (2 shorter events, 0.0 us)
Async XLA Ops:
  7.2 415.0 %copy-start = (bf16[512,1024]{1,0:T(8,128)(2,1)S(1)}, bf16[512,1024]{1,0:T(8,128)(2,1)}, u32[]{:S(2)}) copy-start(bf16[512,1024]{1,0:T(8,128)(2,1)} %param.11) | copy-start | bytes 3145732
  7.2 218.4 %copy-start.1 = (bf16[512,1024]{1,0:T(8,128)(2,1)S(1)}, bf16[512,1024]{1,0:T(8,128)(2,1)}, u32[]{:S(2)}) copy-start(bf16[512,1024]{1,0:T(8,128)(2,1)} %param.10) | copy-start | bytes 3145732
  7.2 218.4 %copy-start.3 = (f32[512]{0:T(512)S(1)}, f32[512]{0:T(512)}, u32[]{:S(2)}) copy-start(f32[512]{0:T(512)} %param.9) | copy-start | bytes 6148
  7.2 218.4 %copy-start.2 = (bf16[176,512]{1,0:T(8,128)(2,1)S(1)}, bf16[176,512]{1,0:T(8,128)(2,1)}, u32[]{:S(2)}) copy-start(bf16[176,512]{1,0:T(8,128)(2,1)} %param.7) | copy-start | bytes 540676
  7.2 106.0 %all-gather.3.cloned.1.call-start = ((), (), s32[]{:S(2)}) async-start(), calls=%async_computation.1 | async-start | bytes 11624448 | tf_op jit(solution)/shard_map/all_gather | solution.py:11
  7.9 217.6 %reduce-scatter.2.cloned.1.call-start = ((), (), s32[]{:S(2)}) async-start(), calls=%async_computation.2 | async-start | bytes 3244032 | tf_op jit(solution)/shard_map/reduce_scatter | solution.py:14
  121.7 218.3 %all-reduce.2.cloned.1.call-start = ((), (), s32[]{:S(2)}) async-start(), calls=%async_computation.3 | async-start | bytes 1441792 | tf_op jit(solution)/shard_map/psum | solution.py:18
  227.8 194.4 %all-gather.5.cloned.1.call-start = ((), (), s32[]{:S(2)}) async-start(), calls=%async_computation.4 | async-start | bytes 11894784 | tf_op jit(solution)/shard_map/all_gather | solution.py:22
Sparse Core Ops, SparseCore 0:
  9.8 103.3 all-gather.2
  121.8 103.6 reduce-scatter.1
  228.8 111.2 all-reduce.1
  343.4 78.7 all-gather.4
where the time goes:
time: 618 us; the launch traced here: 617 us
  waiting for transfers between devices  401 us (65%)
  blocking collectives  149 us (24%)
  matrix products  37.1 us (6%)
  other arithmetic  15.8 us (3%)
  between operations  13.8 us (2%)
    psum x1, waiting for transfers between devices, body(): embed_full = lax.psum(partial_embed, 'cent')  112 us
    all_gather x1, waiting for transfers between devices, body(): lax.all_gather(down_weight, 'dp', axis=1, tiled=True)  105 us
    reduce_scatter x1, waiting for transfers between devices, body(): lax.psum_scatter(partial_layer, 'cent', scatter_dimension=1, tiled=True)  104 us
    all_gather x1, waiting for transfers between devices, body(): gathered = lax.all_gather(scaled, 'dp', axis=0, tiled=True)  78.9 us
    pmax x1, blocking collectives, body(): row_max = lax.pmax(local_max, ('dp', 'cent'))  76.1 us
    psum x1, blocking collectives, body(): lax.psum(jnp.sum(jnp.exp(scores - row_max[:, None]), axis=1), ('dp', 'cen...  73.3 us
    dot_general x1, matrix products, body(): lax.dot_general(prob_low, gathered, (((0,), (0,)), ((), ())), preferred_e...  13.3 us
    dot_general x1, matrix products, body(): lax.dot_general(gathered, centroids, (((1,), (1,)), ((), ())), preferred_...  13.2 us
  transfers between devices with their start and end apart: 4, of which 4 were waited for; matrix products, arithmetic and copies ran while one was open for 0% of the time, Pallas kernels for 0%

commit v1 on v0

--- a/solution.py
+++ b/solution.py
@@ -29,7 +29,9 @@
     )
     local_max = jnp.max(scores, axis=1)
     row_max = lax.pmax(local_max, ("dp", "cent"))
-    row_total = lax.psum(jnp.sum(jnp.exp(scores - row_max[:, None]), axis=1), ("dp", "cent"))
+    row_total = lax.psum(
+        lax.psum(jnp.sum(jnp.exp(scores - row_max[:, None]), axis=1), "cent"), "dp"
+    )
     log_total = row_max + jnp.log(row_total)
     probability = jnp.exp(scores - log_total[:, None])
     scale_up = centroids.shape[0] * lax.axis_size("dp") * lax.axis_size("cent") / gathered.shape[0]

time: 618 us -> 725 us (1.17)
  blocking collectives: 149 us -> 254 us
    psum x1 -> x2, blocking collectives: 73.3 us -> 178 us  [the longest x1 135 us: body(): lax.psum(lax.psum(jnp.sum(jnp.exp(scores - row_max[:, None]), axis=1), 'c...]
where the time goes in v1:
time: 725 us; the launch traced here: 722 us
  waiting for transfers between devices  401 us (55%)
  blocking collectives  254 us (35%)
  matrix products  37.1 us (5%)
  other arithmetic  15.8 us (2%)
  between operations  13.8 us (2%)
    psum x1, blocking collectives, body(): lax.psum(lax.psum(jnp.sum(jnp.exp(scores - row_max[:, None]), axis=1), 'c...  135 us
    psum x1, waiting for transfers between devices, body(): embed_full = lax.psum(partial_embed, 'cent')  112 us
    all_gather x1, waiting for transfers between devices, body(): lax.all_gather(down_weight, 'dp', axis=1, tiled=True)  105 us
    reduce_scatter x1, waiting for transfers between devices, body(): lax.psum_scatter(partial_layer, 'cent', scatter_dimension=1, tiled=True)  104 us
    all_gather x1, waiting for transfers between devices, body(): gathered = lax.all_gather(scaled, 'dp', axis=0, tiled=True)  78.9 us
    pmax x1, blocking collectives, body(): row_max = lax.pmax(local_max, ('dp', 'cent'))  76.1 us
    psum x1, blocking collectives, body(): lax.psum(jnp.sum(jnp.exp(scores - row_max[:, None]), axis=1), 'cent')  43 us
  transfers between devices with their start and end apart: 4, of which 4 were waited for; matrix products, arithmetic and copies ran while one was open for 0% of the time, Pallas kernels for 0%

profile of v1, /device:TPU:1, one launch (start us, length us, event | category | flops | bytes accessed | tf_op | source)
XLA Modules:
  0.0 721.9 jit_solution(5973930479239009705)
XLA Ops:
  7.2 0.0 copy-start
  7.2 0.0 copy-start.1
  7.2 0.0 copy-start.3
  7.2 0.0 copy-start.2
  7.2 0.0 all-gather.3.cloned.1.call-start
  7.3 0.7 all-gather.3.cloned.1.call-update
  7.9 0.0 reduce-scatter.2.cloned.1.call-start
  8.0 105.2 %all-gather.3.cloned.1.call-done = bf16[1376,4096]{1,0:T(8,128)(2,1)} async-done(((bf16[1376,128]{1,0:T(8,128)(2,1)}), bf16[1376,4096]{1,0:T(8,128)(2,1)}) %all-gather.3.cloned.1.call-update) | async-done | bytes 11272208 | tf_op jit(solution)/shard_map/all_gather | solution.py:11
  113.2 8.5 %fusion.11 = f32[176,4096]{1,0:T(8,128)} fusion(bf16[176,1376]{1,0:T(8,128)(2,1)} %param.6, bf16[1376,4096]{1,0:T(8,128)(2,1)} %all-gather.3.cloned.1.call-done), kind=kOutput, calls=%fused_computation.17 | convolution fusion | flops 1983905792 | bytes 14640128 | tf_op jit(solution)/shard_map/dot_general | solution.py:9
  121.7 0.0 reduce-scatter.2.cloned.1.call-update
  121.7 0.0 all-reduce.2.cloned.1.call-start
  121.8 103.8 %reduce-scatter.2.cloned.1.call-done = f32[176,512]{1,0:T(8,128)} async-done(((f32[176,4096]{1,0:T(8,128)}), f32[176,512]{1,0:T(8,128)}) %reduce-scatter.2.cloned.1.call-update) | async-done | bytes 360464 | tf_op jit(solution)/shard_map/reduce_scatter | solution.py:14
  225.6 0.0 copy-done.1
  225.6 0.0 copy-done.3
  225.6 0.0 copy-done.2
  225.6 2.2 fusion.8
  227.8 0.0 all-reduce.2.cloned.1.call-update
  227.8 0.0 all-gather.5.cloned.1.call-start
  227.8 112.2 %all-reduce.2.cloned.1.call-done = f32[176,1024]{1,0:T(8,128)} async-done(((f32[176,1024]{1,0:T(8,128)}), f32[176,1024]{1,0:T(8,128)}) %all-reduce.2.cloned.1.call-update) | async-done | bytes 720912 | tf_op jit(solution)/shard_map/psum | solution.py:18
  340.1 1.2 multiply_reduce_fusion
  341.3 2.0 multiply_convert_fusion
  343.3 0.0 all-gather.5.cloned.1.call-update
  343.3 78.9 %all-gather.5.cloned.1.call-done = bf16[5632,1024]{1,0:T(8,128)(2,1)} async-done(((bf16[176,1024]{1,0:T(8,128)(2,1)}), bf16[5632,1024]{1,0:T(8,128)(2,1)}) %all-gather.5.cloned.1.call-update) | async-done | bytes 11534352 | tf_op jit(solution)/shard_map/all_gather | solution.py:22
  422.2 0.0 copy-done
  422.2 13.2 %fusion.10 = (f32[5632]{0:T(1024)S(1)}, f32[5632,512]{0,1:T(8,128)}) fusion(bf16[5632,1024]{1,0:T(8,128)(2,1)} %all-gather.5.cloned.1.call-done, bf16[512,1024]{1,0:T(8,128)(2,1)S(1)} %copy-done), kind=kOutput, calls=%fused_computation.16 | convolution fusion | flops 5911341568 | bytes 24139776 | tf_op jit(solution)/shard_map/dot_general | solution.py:25
  435.3 76.1 %pmax.7 = f32[5632]{0:T(1024)S(1)} all-reduce(f32[5632]{0:T(1024)S(1)} %get-tuple-element.2), channel_id=1, replica_groups=mesh['dp'=32,'cent'=8] {'dp','cent'}, use_global_device_ids=true, to_apply=%region_4.0 | all-reduce | flops 5632 | bytes 45056 | tf_op jit(solution)/shard_map/pmax | solution.py:31
  511.4 6.0 exponential_reduce_fusion
  517.4 43.0 %psum.22 = f32[5632]{0:T(1024)S(1)} all-reduce(f32[5632]{0:T(1024)S(1)} %exponential_reduce_fusion), channel_id=1, replica_groups=mesh['dp'=32,'cent'=8] {'cent'}, use_global_device_ids=true, to_apply=%region_6.0 | all-reduce | flops 5632 | bytes 45056 | tf_op jit(solution)/shard_map/psum | solution.py:33
  560.4 135.1 %psum.23 = f32[5632]{0:T(1024)S(1)} all-reduce(f32[5632]{0:T(1024)S(1)} %psum.22), channel_id=1, replica_groups=mesh['dp'=32,'cent'=8] {'dp'}, use_global_device_ids=true, to_apply=%region_7.0 | all-reduce | flops 5632 | bytes 45056 | tf_op jit(solution)/shard_map/psum | solution.py:32
  695.5 6.0 fusion
  701.5 0.6 broadcast_multiply_fusion
  702.1 13.3 %fusion.5 = f32[512,1024]{1,0:T(8,128)} fusion(bf16[5632,1024]{1,0:T(8,128)(2,1)} %all-gather.5.cloned.1.call-done, f32[5632,512]{0,1:T(8,128)} %get-tuple-element.3, f32[5632]{0:T(1024)S(1)} %log_add_fusion), kind=kOutput, calls=%fused_computation.7 | convolution fusion | flops 5911871488 | bytes 25188352 | tf_op jit(solution)/shard_map/dot_general | solution.py:40
  (2 shorter events, 0.0 us)
Async XLA Ops:
  7.2 415.0 %copy-start = (bf16[512,1024]{1,0:T(8,128)(2,1)S(1)}, bf16[512,1024]{1,0:T(8,128)(2,1)}, u32[]{:S(2)}) copy-start(bf16[512,1024]{1,0:T(8,128)(2,1)} %param.11) | copy-start | bytes 3145732
  7.2 218.4 %copy-start.1 = (bf16[512,1024]{1,0:T(8,128)(2,1)S(1)}, bf16[512,1024]{1,0:T(8,128)(2,1)}, u32[]{:S(2)}) copy-start(bf16[512,1024]{1,0:T(8,128)(2,1)} %param.10) | copy-start | bytes 3145732
  7.2 218.4 %copy-start.3 = (f32[512]{0:T(512)S(1)}, f32[512]{0:T(512)}, u32[]{:S(2)}) copy-start(f32[512]{0:T(512)} %param.9) | copy-start | bytes 6148
  7.2 218.4 %copy-start.2 = (bf16[176,512]{1,0:T(8,128)(2,1)S(1)}, bf16[176,512]{1,0:T(8,128)(2,1)}, u32[]{:S(2)}) copy-start(bf16[176,512]{1,0:T(8,128)(2,1)} %param.7) | copy-start | bytes 540676
  7.2 106.0 %all-gather.3.cloned.1.call-start = ((), (), s32[]{:S(2)}) async-start(), calls=%async_computation.1 | async-start | bytes 11624448 | tf_op jit(solution)/shard_map/all_gather | solution.py:11
  7.9 217.6 %reduce-scatter.2.cloned.1.call-start = ((), (), s32[]{:S(2)}) async-start(), calls=%async_computation.2 | async-start | bytes 3244032 | tf_op jit(solution)/shard_map/reduce_scatter | solution.py:14
  121.7 218.3 %all-reduce.2.cloned.1.call-start = ((), (), s32[]{:S(2)}) async-start(), calls=%async_computation.3 | async-start | bytes 1441792 | tf_op jit(solution)/shard_map/psum | solution.py:18
  227.8 194.4 %all-gather.5.cloned.1.call-start = ((), (), s32[]{:S(2)}) async-start(), calls=%async_computation.4 | async-start | bytes 11894784 | tf_op jit(solution)/shard_map/all_gather | solution.py:22
Sparse Core Ops, SparseCore 0:
  9.8 103.3 all-gather.2
  121.8 103.6 reduce-scatter.1
  228.8 111.2 all-reduce.1
  343.4 78.7 all-gather.4
